TPU v7x, 32 devices: a whole 2x2x4 slice. The times are simulated.
32 devices in a mesh: grp: 2 (over core), seq: 8 (over z, y), tp: 2 (over x).
Axes of the slice: x: 2, y: 2, z: 4, core: 2. Of those that a mesh axis runs over, the one named last changes fastest.
Arguments:
- prompt_states: bfloat16 [2, 16384, 4096], P(None, ('grp', 'seq'), 'tp'), may hold values from -40 to 40
- q_weight: bfloat16 [4096, 16, 128], P(None, 'tp'), may hold values from -0.09375 to 0.09375
- kv_weight: bfloat16 [4096, 2, 4, 128], P(None, None, 'tp'), may hold values from -0.09375 to 0.09375
- lengths: int32 [2], replicated, may hold values from 4096 to 16384, as said below
- sink_positions: int32 [2, 4], replicated, may hold values from 0 to 2047
Outputs:
- attended: bfloat16 [2, 16384, 2048], P(None, ('grp', 'seq'), 'tp')
- kv_cache: bfloat16 [2, 4, 2, 8, 1024, 256], P(None, ('tp', 'grp'), None, 'seq')
Inputs may be any that keep to these rules, and one draw needn't show every extreme that they name: `lengths`: at least one request has length 16384.
All inputs are finite; a program needn't handle non-finite values.
Results may differ from a plain program's by a relative error of at most 0.0065.
Values may be sent and summed in bfloat16 or wider, within the bound.
No kernel may reach another device: no remote copies, remote signals or barrier semaphores. Data moves between devices by JAX's collectives and lax.ppermute only.
A program may use at most 512 MiB of HBM per device.

v0:
```python
import math
import jax
import jax.numpy as jnp
from jax import lax
from jax.sharding import PartitionSpec as P

WINDOW = 4096
ROPE_BASE = 10000.0
NEG_FILL = -1e30


def shifted(block, axis, distance):
    devices = range(lax.axis_size(axis))
    route = [(i - distance, i) for i in devices if i - distance in devices]
    return lax.ppermute(block, axis, route)


def rotate(vectors, positions):
    head_dim = vectors.shape[-1]
    half_dim = head_dim // 2
    ladder = jnp.arange(half_dim, dtype=jnp.float32) * (2.0 / head_dim)
    inv_freq = jnp.exp(-math.log(ROPE_BASE) * ladder)
    angles = positions.astype(jnp.float32)[:, None] * inv_freq[None, :]
    cosine = jnp.cos(angles)[None, :, None, :]
    sine_part = jnp.sin(angles)[None, :, None, :]
    lead_half = vectors[..., :half_dim]
    tail_half = vectors[..., half_dim:]
    return jnp.concatenate(
        [lead_half * cosine - tail_half * sine_part, tail_half * cosine + lead_half * sine_part],
        axis=-1,
    )


def window_mask(key_pos, query_pos, lengths, sink_positions):
    sink_flag = jnp.any(key_pos[:, :, None] == sink_positions[:, None, :], axis=2)
    distance = query_pos[None, :, None] - key_pos[:, None, :]
    in_window = distance < WINDOW
    return (
        (distance >= 0)
        & (key_pos[:, None, :] >= 0)
        & (key_pos[:, None, :] < lengths[:, None, None])
        & (in_window | sink_flag[:, None, :])
    )


def attend(carried, in_block, visible, queries, inv_root):
    running, sums_now, weighted = carried
    scores = (
        jnp.einsum(
            "rqhgd,rkhd->rhgqk", queries, in_block[:, :, 0], preferred_element_type=jnp.float32
        )
        * inv_root
    )
    masked = visible[:, None, None]
    scores = jnp.where(masked, scores, NEG_FILL)
    new_max = jnp.maximum(running, jnp.max(scores, axis=-1))
    weights = jnp.where(masked, jnp.exp(scores - new_max[..., None]), 0.0)
    factor = jnp.exp(running - new_max)
    sums_now = sums_now * factor + jnp.sum(weights, axis=-1)
    weight_rows = weights.astype(jnp.bfloat16)
    weighted = weighted * factor[..., None] + jnp.einsum(
        "rhgqk,rkhd->rhgqd", weight_rows, in_block[:, :, 1], preferred_element_type=jnp.float32
    )
    return (new_max, sums_now, weighted)


def per_device(prompt_states, q_weight, kv_weight, lengths, sink_positions):
    num_reqs, slab_len, half_width = prompt_states.shape
    model_width, local_heads, head_dim = q_weight.shape
    kv_local = kv_weight.shape[2]
    share_count = local_heads // kv_local
    token_count = num_reqs * slab_len
    q_matrix = q_weight.reshape(model_width, local_heads * head_dim)
    kv_matrix = kv_weight.reshape(model_width, 2 * kv_local * head_dim)
    shard_part = lax.all_gather(prompt_states, "tp", axis=2, tiled=True)
    columns = shard_part.shape[2]
    flattened = shard_part.reshape(token_count, columns)
    query_raw = jnp.dot(flattened, q_matrix, preferred_element_type=jnp.float32)
    kv_raw = jnp.dot(flattened, kv_matrix, preferred_element_type=jnp.float32)
    device_index = lax.axis_index(("grp", "seq"))
    span_slabs = (WINDOW - 1) // slab_len + 1
    anchor = device_index * slab_len
    positions = anchor + jnp.arange(slab_len, dtype=jnp.int32)
    queries = rotate(
        query_raw.reshape(num_reqs, slab_len, local_heads, head_dim), positions
    ).astype(jnp.bfloat16)
    queries = queries.reshape(num_reqs, slab_len, kv_local, share_count, head_dim)
    kv_raw = kv_raw.reshape(num_reqs, slab_len, 2, kv_local, head_dim)
    key_rows = rotate(kv_raw[:, :, 0], positions).astype(jnp.bfloat16)
    values = kv_raw[:, :, 1].astype(jnp.bfloat16)
    own_rows = jnp.stack([key_rows, values], axis=2)
    inv_root = 1.0 / math.sqrt(head_dim)

    def fold_block(carried, in_block, key_line):
        key_pos = jnp.broadcast_to(key_line[None, :], (num_reqs, key_line.shape[0]))
        return attend(
            carried,
            in_block,
            window_mask(key_pos, positions, lengths, sink_positions),
            queries,
            inv_root,
        )

    carried = (
        jnp.full((num_reqs, kv_local, share_count, slab_len), NEG_FILL, jnp.float32),
        jnp.zeros((num_reqs, kv_local, share_count, slab_len), jnp.float32),
        jnp.zeros((num_reqs, kv_local, share_count, slab_len, head_dim), jnp.float32),
    )
    carried = fold_block(carried, own_rows, positions)
    held_rows = own_rows
    held_pos = positions
    stride = 1
    while stride < span_slabs:
        incoming = shifted(held_rows, ("grp", "seq"), stride)
        incoming_pos = held_pos - stride * slab_len
        carried = fold_block(carried, incoming, incoming_pos)
        if stride * 2 < span_slabs:
            held_rows = jnp.concatenate([incoming, held_rows], axis=1)
            held_pos = jnp.concatenate([incoming_pos, held_pos])
        stride = stride * 2
    farthest = shifted(own_rows, ("grp", "seq"), span_slabs)
    carried = fold_block(carried, farthest, positions - span_slabs * slab_len)
    sink_hits = (sink_positions[:, :, None] == positions[None, None, :]).astype(jnp.bfloat16)
    sink_terms = jnp.einsum(
        "rks,rsxhd->rkxhd", sink_hits, own_rows, preferred_element_type=jnp.float32
    )
    sink_block = lax.psum(sink_terms, ("grp", "seq")).astype(jnp.bfloat16)
    mark_count = sink_positions.shape[1]
    earlier = jnp.arange(mark_count)[None, :] < jnp.arange(mark_count)[:, None]
    repeated = jnp.any(
        (sink_positions[:, :, None] == sink_positions[:, None, :]) & earlier[None], axis=2
    )
    uncovered = sink_positions < (device_index - span_slabs) * slab_len
    sink_usable = ~repeated & uncovered & (sink_positions < lengths[:, None])
    sink_visible = sink_usable[:, None, :] & (
        sink_positions[:, None, :] <= positions[None, :, None]
    )
    carried = attend(carried, sink_block, sink_visible, queries, inv_root)
    running, sums_now, weighted = carried
    mixed = weighted / sums_now[..., None]
    mixed = jnp.transpose(mixed, (0, 3, 1, 2, 4)).reshape(
        num_reqs, slab_len, local_heads * head_dim
    )
    live_rows = positions[None, :] < lengths[:, None]
    attended = jnp.where(live_rows[:, :, None], mixed, 0.0).astype(jnp.bfloat16)
    cache_rows = jnp.concatenate([key_rows, values], axis=-1)
    cache_rows = jnp.where(live_rows[:, :, None, None], cache_rows, jnp.zeros_like(cache_rows))
    pieces = jnp.transpose(cache_rows, (0, 2, 1, 3)).reshape(
        num_reqs, kv_local, 1, 1, slab_len, 2 * head_dim
    )
    kv_cache = lax.all_to_all(pieces, "grp", split_axis=1, concat_axis=2, tiled=True)
    return (attended, kv_cache)


def solution(mesh):
    placed = (
        P(None, ("grp", "seq"), "tp"),
        P(None, "tp", None),
        P(None, None, "tp", None),
        P(),
        P(),
    )
    return jax.shard_map(
        per_device,
        mesh=mesh,
        in_specs=placed,
        out_specs=(P(None, ("grp", "seq"), "tp"), P(None, ("tp", "grp"), None, "seq", None, None)),
        check_vma=False,
    )
```

profile of v0, /device:TPU:0, one launch (start us, length us, event | category | flops | bytes accessed | tf_op | source)
XLA Modules:
  0.0 840.8 jit_solution(16857945234379509448)
XLA Ops:
  7.9 7.2 reshape.486
  15.1 6.7 copy.42
  21.8 11.3 %copy.89 = bf16[512,8,8,128]{3,1,2,0:T(8,128)(2,1)} copy(bf16[512,8,8,128]{3,2,1,0:T(8,128)(2,1)} %bitcast.331) | data formatting | bytes 16777216
  33.1 11.6 %copy.44 = bf16[1024,4096]{1,0:T(8,128)(2,1)} copy(bf16[1024,4096]{0,1:T(8,128)(2,1)} %bitcast.323) | data formatting | bytes 16777216 | tf_op jit(solution)/shard_map/dot_general | solution.py:78
  47.3 6.6 fusion.30
  54.0 9.3 %fusion.39 = (pred[2,1024,1024]{1,2,0:T(8,128)(4,1)S(1)}, pred[2,1024,1024]{1,2,0:T(8,128)(4,1)}, pred[2,1024,1024]{1,2,0:T(8,128)(4,1)}) fusion(s32[1024]{0:T(1024)S(1)} %iota_add_fusion, pred[1024]{0:T(1024)(128)(4,1)S(1)} %get-tuple-element.47, pred[2,1024]{1,0:T(4,128)(4,1)S(1)} %get-tuple-element.10, pred[2,1024]{1,0:T(4,128)(4,1)S(1)} %get-tuple-element.32, ...), kind=kLoop, calls=%fused_computation.58 | loop fusion | flops 44040192 | bytes 6319104 | tf_op jit(solution)/shard_map/and | solution.py:39
  63.2 147.9 %all-gather.2.cloned.1.call-done = bf16[2,1024,4096]{2,1,0:T(8,128)(2,1)} async-done(((bf16[2,1024,2048]{2,1,0:T(8,128)(2,1)}), bf16[2,1024,4096]{2,1,0:T(8,128)(2,1)}) %all-gather.2.cloned.1.call-update) | async-done | bytes 16777232 | tf_op jit(solution)/shard_map/all_gather | solution.py:75
  211.1 13.1 %fusion.26 = f32[2,1024,2,2,128]{1,4,3,2,0:T(8,128)S(1)} fusion(bf16[2,2,128,4096,1]{3,2,1,0,4:T(8,128)(2,1)} %bitcast.335, bf16[2,1024,4096]{2,1,0:T(8,128)(2,1)} %all-gather.2.cloned.1.call-done), kind=kOutput, calls=%fused_computation.32 | convolution fusion | flops 8589934592 | bytes 25165824 | tf_op jit(solution)/shard_map/dot_general | solution.py:79
  239.5 21.0 %fusion.24 = f32[2,1024,8,128]{1,3,2,0:T(8,128)S(1)} fusion(bf16[8,128,4096,1]{2,1,0,3:T(8,128)(2,1)S(1)} %bitcast.334, bf16[2,1024,4096]{2,1,0:T(8,128)(2,1)} %all-gather.2.cloned.1.call-done), kind=kOutput, calls=%fused_computation.30 | convolution fusion | flops 17179869184 | bytes 33554432 | tf_op jit(solution)/shard_map/dot_general | solution.py:78
  288.6 23.9 %fusion.6 = (f32[2,2,4,1024]{3,2,1,0:T(4,128)S(1)}, f32[2,2,1024,1024,4]{3,2,4,1,0:T(8,128)}) fusion(pred[2,1024,1024]{1,2,0:T(8,128)(4,1)S(1)} %get-tuple-element.29, bf16[2,1024,2,4,128]{4,1,3,2,0:T(8,128)(2,1)S(1)} %pad_maximum_fusion, bf16[2,1024,2,64]{1,3,2,0:T(8,128)(2,1)S(1)} %get-tuple-element.22, bf16[2,1024,2,64]{1,3,2,0:T(8,128)(2,1)S(1)} %get-tuple-element.21), kind=kOutput, calls=%fused_computation.13 | convolution fusion | flops 4347379712 | bytes 74514432 | tf_op jit(solution)/shard_map/rqhgd,rkhd->rhgqk/dot_general | solution.py:49
  318.7 99.8 %psum.7 = bf16[2,4,2,2,128]{4,1,3,2,0:T(4,128)(2,1)S(1)} all-reduce(f32[2,4,2,2,128]{4,1,3,2,0:T(4,128)S(1)} %fusion.76), channel_id=1, replica_groups=mesh['grp'=2,'seq'=8,'tp'=2] {'grp','seq'}, use_global_device_ids=true, to_apply=%region_9.10 | all-reduce | flops 4096 | bytes 24576 | tf_op jit(solution)/shard_map/psum | solution.py:127
  430.0 25.6 %fusion.7 = (f32[2,2,4,1024]{3,2,1,0:T(4,128)S(1)}, f32[2,2,1024,1024,4]{3,2,4,1,0:T(8,128)}) fusion(pred[2,1024,1024]{1,2,0:T(8,128)(4,1)} %get-tuple-element.31, bf16[2,1024,2,4,128]{4,1,3,2,0:T(8,128)(2,1)S(1)} %copy-done.1, bf16[2,1024,2,2,128]{1,4,3,2,0:T(8,128)(2,1)} %collective-permute-done), kind=kOutput, calls=%fused_computation.14 | convolution fusion | flops 4345282560 | bytes 74514432 | tf_op jit(solution)/shard_map/rqhgd,rkhd->rhgqk/dot_general | solution.py:49
  455.6 25.0 %fusion.8 = (f32[2,2,4,1024]{3,2,1,0:T(4,128)S(1)}, f32[2,2,1024,1024,4]{3,2,4,1,0:T(8,128)}) fusion(pred[2,1024,1024]{1,2,0:T(8,128)(4,1)S(1)} %copy-done.3, bf16[2,1024,2,4,128]{4,1,3,2,0:T(8,128)(2,1)S(1)} %copy-done.1, bf16[2,1024,2,2,128]{1,4,3,2,0:T(8,128)(2,1)} %collective-permute-done.2), kind=kOutput, calls=%fused_computation.15 | convolution fusion | flops 4345282560 | bytes 74514432 | tf_op jit(solution)/shard_map/rqhgd,rkhd->rhgqk/dot_general | solution.py:49
  480.6 38.3 %collective-permute-done.1 = bf16[2,2048,2,2,128]{1,4,3,2,0:T(8,128)(2,1)} collective-permute-done((bf16[2,2048,2,2,128]{1,4,3,2,0:T(8,128)(2,1)}, bf16[2,2048,2,2,128]{1,4,3,2,0:T(8,128)(2,1)}, u32[]{:S(2)}, u32[]{:S(2)}) %collective-permute-start.1) | collective-permute-done | bytes 4194336 | tf_op jit(solution)/shard_map/ppermute | solution.py:15
  518.9 48.3 %fusion = (f32[2,2,4,1024]{3,2,1,0:T(4,128)S(1)}, f32[2,2,2048,1024,4]{3,2,4,1,0:T(8,128)}) fusion(pred[2,1024,2048]{1,2,0:T(8,128)(4,1)} %fusion.30, bf16[2,1024,2,4,128]{4,1,3,2,0:T(8,128)(2,1)} %copy-done, bf16[2,2048,2,2,128]{1,4,3,2,0:T(8,128)(2,1)} %collective-permute-done.1), kind=kOutput, calls=%fused_computation.2 | convolution fusion | flops 8690581504 | bytes 144769024 | tf_op jit(solution)/shard_map/rqhgd,rkhd->rhgqk/dot_general | solution.py:49
  567.3 21.7 %fusion.9 = f32[2,2,4,1024]{3,2,1,0:T(4,128)S(1)} fusion(f32[2,2,1024,1024,4]{3,2,4,1,0:T(8,128)} %get-tuple-element.44, f32[2,2,4,1024]{3,2,1,0:T(4,128)S(1)} %get-tuple-element.25, pred[2,1024,1024]{1,2,0:T(8,128)(4,1)S(1)} %get-tuple-element.29), kind=kLoop, calls=%fused_computation.16 | loop fusion | flops 83869696 | bytes 69337088 | tf_op jit(solution)/shard_map/reduce_sum | solution.py:59
  589.0 29.2 %fusion.19 = f32[2,2,4,1024,128]{3,4,2,1,0:T(8,128)} fusion(f32[2,2,1024,1024,4]{3,2,4,1,0:T(8,128)} %get-tuple-element.44, f32[2,2,4,1024]{3,2,1,0:T(4,128)S(1)} %get-tuple-element.25, pred[2,1024,1024]{1,2,0:T(8,128)(4,1)S(1)} %get-tuple-element.29, f32[2,1024,2,2,128]{1,4,3,2,0:T(8,128)} %copy-done.6), kind=kOutput, calls=%fused_computation.24 | convolution fusion | flops 4378853376 | bytes 78708736 | tf_op jit(solution)/shard_map/rhgqk,rkhd->rhgqd/dot_general | solution.py:61
  623.1 21.7 %fusion.11 = f32[2,2,4,1024]{3,2,1,0:T(4,128)S(1)} fusion(f32[2,2,1024,1024,4]{3,2,4,1,0:T(8,128)} %get-tuple-element.42, f32[2,2,4,1024]{3,2,1,0:T(4,128)S(1)} %get-tuple-element.18, pred[2,1024,1024]{1,2,0:T(8,128)(4,1)S(1)} %copy-done.5), kind=kLoop, calls=%fused_computation.18 | loop fusion | flops 83869696 | bytes 69337088 | tf_op jit(solution)/shard_map/reduce_sum | solution.py:59
  644.8 42.6 %fusion.1 = f32[2,2,4,1024]{3,2,1,0:T(4,128)S(1)} fusion(f32[2,2,2048,1024,4]{3,2,4,1,0:T(8,128)} %get-tuple-element.40, f32[2,2,4,1024]{3,2,1,0:T(4,128)S(1)} %get-tuple-element.17, pred[2,1024,2048]{1,2,0:T(8,128)(4,1)} %fusion.30), kind=kLoop, calls=%fused_computation.3 | loop fusion | flops 167755776 | bytes 138543104 | tf_op jit(solution)/shard_map/reduce_sum | solution.py:59
  687.4 21.7 %fusion.13 = f32[2,2,4,1024]{3,2,1,0:T(4,128)S(1)} fusion(f32[2,2,1024,1024,4]{3,2,4,1,0:T(8,128)} %get-tuple-element.38, f32[2,2,4,1024]{3,2,1,0:T(4,128)S(1)} %get-tuple-element.16, pred[2,1024,1024]{1,2,0:T(8,128)(4,1)S(1)} %copy-done.4), kind=kLoop, calls=%fused_computation.20 | loop fusion | flops 83869696 | bytes 69337088 | tf_op jit(solution)/shard_map/reduce_sum | solution.py:59
  709.3 29.0 %fusion.17 = f32[2,2,4,1024,128]{3,4,2,1,0:T(8,128)} fusion(f32[2,2,1024,1024,4]{3,2,4,1,0:T(8,128)} %get-tuple-element.42, f32[2,2,4,1024]{3,2,1,0:T(4,128)S(1)} %get-tuple-element.18, pred[2,1024,1024]{1,2,0:T(8,128)(4,1)} %get-tuple-element.31, bf16[2,1024,2,2,128]{1,4,3,2,0:T(8,128)(2,1)} %collective-permute-done), kind=kOutput, calls=%fused_computation.23 | convolution fusion | flops 4378853376 | bytes 78708736 | tf_op jit(solution)/shard_map/rhgqk,rkhd->rhgqd/dot_general | solution.py:61
  738.2 50.0 %fusion.3 = f32[2,2,4,1024,128]{3,4,2,1,0:T(8,128)} fusion(f32[2,2,2048,1024,4]{3,2,4,1,0:T(8,128)} %get-tuple-element.40, f32[2,2,4,1024]{3,2,1,0:T(4,128)S(1)} %get-tuple-element.17, pred[2,1024,2048]{1,2,0:T(8,128)(4,1)} %fusion.30, bf16[2,2048,2,2,128]{1,4,3,2,0:T(8,128)(2,1)} %collective-permute-done.1), kind=kOutput, calls=%fused_computation.11 | convolution fusion | flops 8757706752 | bytes 148963328 | tf_op jit(solution)/shard_map/rhgqk,rkhd->rhgqd/dot_general | solution.py:61
  788.2 35.3 %fusion.32 = bf16[2,1024,2,4,128]{1,4,3,2,0:T(8,128)(2,1)} fusion(f32[2,2,4,1024,128]{3,4,2,1,0:T(8,128)} %fusion.63, f32[2,2,4,1024,128]{3,4,2,1,0:T(8,128)} %fusion.3, f32[2,2,4,1024,128]{3,4,2,1,0:T(8,128)} %fusion.17, f32[2,2,4,1024,128]{3,4,2,1,0:T(8,128)} %fusion.19, f32[2,1024,2,4]{1,3,2,0:T(4,128)S(1)} %get-tuple-element.11, ...), kind=kOutput, calls=%fused_computation.46 | convolution fusion | flops 4401922048 | bytes 108462080 | tf_op jit(solution)/shard_map/rhgqk,rkhd->rhgqd/dot_general | solution.py:61
  823.5 6.2 copy.57
  (84 shorter events, 73.3 us)
Async XLA Ops:
  7.2 204.0 %all-gather.2.cloned.1.call-start = ((), (), s32[]{:S(2)}) async-start(), calls=%async_computation.1 | async-start | bytes 25165824 | tf_op jit(solution)/shard_map/all_gather | solution.py:75
  33.1 11.7 %copy-start.13 = (s32[2,4]{1,0:T(2,128)S(1)}, s32[2,4]{1,0:T(2,128)}, u32[]{:S(2)}) copy-start(s32[2,4]{1,0:T(2,128)} %param.9) | copy-start | bytes 100
  33.1 12.0 %copy-start.16 = (s32[2]{0:T(128)S(1)}, s32[2]{0:T(128)}, u32[]{:S(2)}) copy-start(s32[2]{0:T(128)} %param.8) | copy-start | bytes 28
  45.4 373.1 %copy-start.9 = (pred[2,1024,4]{1,2,0:T(4,128)(4,1)}, pred[2,1024,4]{1,2,0:T(4,128)(4,1)S(1)}, u32[]{:S(2)}) copy-start(pred[2,1024,4]{1,2,0:T(4,128)(4,1)S(1)} %get-tuple-element.26) | copy-start | bytes 24580
  45.5 228.2 %copy-start.11 = (pred[2,1024]{1,0:T(4,128)(4,1)}, pred[2,1024]{1,0:T(4,128)(4,1)S(1)}, u32[]{:S(2)}) copy-start(pred[2,1024]{1,0:T(4,128)(4,1)S(1)} %get-tuple-element.32) | copy-start | bytes 6148
  211.1 13.5 %copy-start.7 = (f32[1024,64]{0,1:T(8,128)S(1)}, f32[1024,64]{0,1:T(8,128)}, u32[]{:S(2)}) copy-start(f32[1024,64]{0,1:T(8,128)} %get-tuple-element.28) | copy-start | bytes 786436
  224.3 15.2 %copy-start.6 = (f32[2,1024,2,2,128]{1,4,3,2,0:T(8,128)}, f32[2,1024,2,2,128]{1,4,3,2,0:T(8,128)S(1)}, u32[]{:S(2)}) copy-start(f32[2,1024,2,2,128]{1,4,3,2,0:T(8,128)S(1)} %fusion.26) | copy-start | bytes 12582916
  224.3 15.2 %slice-start = ((s8[8388608]{0:T(1024)(128)(4,1)}), s8[4194304]{0:T(1024)(128)(4,1)S(1)}, s32[]{:S(2)}) async-start(s8[8388608]{0:T(1024)(128)(4,1)} %bitcast.332), calls=%async_computation.2 | async-start | bytes 8388608
  224.6 2.3 copy-start.2
  224.6 14.9 %slice-start.1 = ((s8[8388608]{0:T(1024)(128)(4,1)}), s8[4194304]{0:T(1024)(128)(4,1)S(1)}, s32[]{:S(2)}) async-start(s8[8388608]{0:T(1024)(128)(4,1)} %bitcast.332), calls=%async_computation.3 | async-start | bytes 8388608
  228.5 194.2 %collective-permute-start = (bf16[2,1024,2,2,128]{1,4,3,2,0:T(8,128)(2,1)}, bf16[2,1024,2,2,128]{1,4,3,2,0:T(8,128)(2,1)}, u32[]{:S(2)}, u32[]{:S(2)}) collective-permute-start(bf16[2,1024,2,2,128]{1,4,3,2,0:T(8,128)(2,1)} %pad_maximum_fusion.1), channel_id=1, source_target_pairs={{0,2},{2,4},{4,6},{6,8},{8,10},{10,12},{12,14},{14,16},{16,18},{18... | collective-permute-start | bytes 6291464 | tf_op jit(solution)/shard_map/ppermute | solution.py:15
  233.5 222.1 %collective-permute-start.2 = (bf16[2,1024,2,2,128]{1,4,3,2,0:T(8,128)(2,1)}, bf16[2,1024,2,2,128]{1,4,3,2,0:T(8,128)(2,1)}, u32[]{:S(2)}, u32[]{:S(2)}) collective-permute-start(bf16[2,1024,2,2,128]{1,4,3,2,0:T(8,128)(2,1)} %pad_maximum_fusion.1), channel_id=1, source_target_pairs={{0,8},{2,10},{4,12},{6,14},{8,16},{10,18},{12,20},{14,22},{16,24},... | collective-permute-start | bytes 6291464 | tf_op jit(solution)/shard_map/ppermute | solution.py:15
  276.9 35.6 %all-to-all-start = ((bf16[2,2,1,1,1024,256]{4,5,0,3,2,1:T(8,128)(2,1)}), bf16[2,2,1,1,1024,256]{4,5,0,3,2,1:T(8,128)(2,1)}, u32[]{:S(2)}, u32[]{:S(2)}) async-start(bf16[2,2,1,1,1024,256]{4,5,0,3,2,1:T(8,128)(2,1)} %copy.58), calls=%async_computation | async-start | bytes 4194304 | tf_op jit(solution)/shard_map/all_to_all | solution.py:151
  286.6 2.0 copy-start
  418.5 37.1 %copy-start.14 = (bf16[2,4,2,2,128]{4,1,3,2,0:T(4,128)(2,1)}, bf16[2,4,2,2,128]{4,1,3,2,0:T(4,128)(2,1)S(1)}, u32[]{:S(2)}) copy-start(bf16[2,4,2,2,128]{4,1,3,2,0:T(4,128)(2,1)S(1)} %psum.7) | copy-start | bytes 24580
  418.5 11.6 %copy-start.1 = (bf16[2,1024,2,4,128]{4,1,3,2,0:T(8,128)(2,1)S(1)}, bf16[2,1024,2,4,128]{4,1,3,2,0:T(8,128)(2,1)}, u32[]{:S(2)}) copy-start(bf16[2,1024,2,4,128]{4,1,3,2,0:T(8,128)(2,1)} %copy-done) | copy-start | bytes 12582916
  426.3 92.6 %collective-permute-start.1 = (bf16[2,2048,2,2,128]{1,4,3,2,0:T(8,128)(2,1)}, bf16[2,2048,2,2,128]{1,4,3,2,0:T(8,128)(2,1)}, u32[]{:S(2)}, u32[]{:S(2)}) collective-permute-start(bf16[2,2048,2,2,128]{1,4,3,2,0:T(8,128)(2,1)} %maximum_maximum_fusion), channel_id=1, source_target_pairs={{0,4},{2,6},{4,8},{6,10},{8,12},{10,14},{12,16},{14,18},{16,20},{1... | collective-permute-start | bytes 12582920 | tf_op jit(solution)/shard_map/ppermute | solution.py:15
  430.0 25.6 %copy-start.3 = (pred[2,1024,1024]{1,2,0:T(8,128)(4,1)S(1)}, pred[2,1024,1024]{1,2,0:T(8,128)(4,1)}, u32[]{:S(2)}) copy-start(pred[2,1024,1024]{1,2,0:T(8,128)(4,1)} %get-tuple-element.30) | copy-start | bytes 6291460
  589.0 29.3 %copy-start.8 = (f32[2,2,4,1024,4]{3,4,2,1,0:T(4,128)S(1)}, f32[2,2,4,1024,4]{3,4,2,1,0:T(4,128)}, u32[]{:S(2)}) copy-start(f32[2,2,4,1024,4]{3,4,2,1,0:T(4,128)} %get-tuple-element.36) | copy-start | bytes 786436
  589.0 29.3 %copy-start.10 = (pred[2,1024,4]{1,2,0:T(4,128)(4,1)S(1)}, pred[2,1024,4]{1,2,0:T(4,128)(4,1)}, u32[]{:S(2)}) copy-start(pred[2,1024,4]{1,2,0:T(4,128)(4,1)} %copy-done.9) | copy-start | bytes 24580
  589.0 29.5 %copy-start.15 = (bf16[2,4,2,2,128]{4,1,3,2,0:T(4,128)(2,1)S(1)}, bf16[2,4,2,2,128]{4,1,3,2,0:T(4,128)(2,1)}, u32[]{:S(2)}) copy-start(bf16[2,4,2,2,128]{4,1,3,2,0:T(4,128)(2,1)} %copy-done.14) | copy-start | bytes 24580
  618.2 4.9 copy-start.5
  644.8 42.7 %copy-start.4 = (pred[2,1024,1024]{1,2,0:T(8,128)(4,1)S(1)}, pred[2,1024,1024]{1,2,0:T(8,128)(4,1)}, u32[]{:S(2)}) copy-start(pred[2,1024,1024]{1,2,0:T(8,128)(4,1)} %get-tuple-element.30) | copy-start | bytes 6291460
  823.5 6.2 copy-start.12
Sparse Core Ops, SparseCore 0:
  9.5 201.5 all-gather.1
where the time goes:
time: 848 us; the launch traced here: 841 us
  matrix products  311 us (37%)
  waiting for transfers between devices  187 us (22%)
  other arithmetic  146 us (17%)
  blocking collectives  99.8 us (12%)
  local copies, waits for them, and re-layouts  63.4 us (7%)
  starting transfers between devices  18.5 us (2%)
  between operations  14.6 us (2%)
    dot_general x5, matrix products, attend(): jnp.einsum('rhgqk,rkhd->rhgqd', weight_rows, in_block[:, :, 1], preferred...  148 us
    all_gather x1, waiting for transfers between devices, per_device(): shard_part = lax.all_gather(prompt_states, 'tp', axis=2, tiled=True)  148 us
    dot_general x5, matrix products, attend(): jnp.einsum('rqhgd,rkhd->rhgqk', queries, in_block[:, :, 0], preferred_ele...  127 us
    reduce_sum x5, other arithmetic, attend(): sums_now = sums_now * factor + jnp.sum(weights, axis=-1)  108 us
    psum x1, blocking collectives, per_device(): sink_block = lax.psum(sink_terms, ('grp', 'seq')).astype(jnp.bfloat16)  99.8 us
    ppermute x3, waiting for transfers between devices, shifted(): return lax.ppermute(block, axis, route)  38.3 us
    dot_general x1, matrix products, per_device(): query_raw = jnp.dot(flattened, q_matrix, preferred_element_type=jnp.float32)  21 us
    unnamed x40, local copies, waits for them, and re-layouts  19.3 us
  transfers between devices with their start and end apart: 5, of which 2 were waited for; matrix products, arithmetic and copies ran while one was open for 22% of the time, Pallas kernels for 0%

commit v1 on v0

--- a/solution.py
+++ b/solution.py
@@ -124,7 +124,7 @@
     sink_terms = jnp.einsum(
         "rks,rsxhd->rkxhd", sink_hits, own_rows, preferred_element_type=jnp.float32
     )
-    sink_block = lax.psum(sink_terms, ("grp", "seq")).astype(jnp.bfloat16)
+    sink_block = jnp.sum(lax.all_gather(sink_terms, ("grp", "seq")), axis=0).astype(jnp.bfloat16)
     mark_count = sink_positions.shape[1]
     earlier = jnp.arange(mark_count)[None, :] < jnp.arange(mark_count)[:, None]
     repeated = jnp.any(

time: 848 us -> 821 us (0.968)
  blocking collectives: 99.8 us -> 72.6 us
    psum x1 -> x0, blocking collectives: 99.8 us -> none  [per_device(): sink_block = lax.psum(sink_terms, ('grp', 'seq')).astype(jnp.bfloat16)]
    all_gather x0 -> x1, blocking collectives: none -> 72.6 us  [per_device(): lax.all_gather(sink_terms, ('grp', 'seq'))]
  transfers between devices with their start and end apart: 5 -> 5, of which waited for: 2 -> 2; matrix products, arithmetic and copies ran while one was open for 22% -> 23% of each run, Pallas kernels for 0% -> 0%
where the time goes in v1:
time: 821 us; the launch traced here: 814 us
  matrix products  311 us (38%)
  waiting for transfers between devices  186 us (23%)
  other arithmetic  146 us (18%)
  blocking collectives  72.6 us (9%)
  local copies, waits for them, and re-layouts  63.4 us (8%)
  starting transfers between devices  19.3 us (2%)
  between operations  14.6 us (2%)
    dot_general x5, matrix products, attend(): jnp.einsum('rhgqk,rkhd->rhgqd', weight_rows, in_block[:, :, 1], preferred...  148 us
    all_gather x1, waiting for transfers between devices, per_device(): shard_part = lax.all_gather(prompt_states, 'tp', axis=2, tiled=True)  148 us
    dot_general x5, matrix products, attend(): jnp.einsum('rqhgd,rkhd->rhgqk', queries, in_block[:, :, 0], preferred_ele...  127 us
    reduce_sum x5, other arithmetic, attend(): sums_now = sums_now * factor + jnp.sum(weights, axis=-1)  108 us
    all_gather x1, blocking collectives, per_device(): lax.all_gather(sink_terms, ('grp', 'seq'))  72.6 us
    ppermute x3, waiting for transfers between devices, shifted(): return lax.ppermute(block, axis, route)  37.3 us
    dot_general x1, matrix products, per_device(): query_raw = jnp.dot(flattened, q_matrix, preferred_element_type=jnp.float32)  21 us
    unnamed x40, local copies, waits for them, and re-layouts  19.3 us
  transfers between devices with their start and end apart: 5, of which 2 were waited for; matrix products, arithmetic and copies ran while one was open for 23% of the time, Pallas kernels for 0%

profile of v1, /device:TPU:0, one launch (start us, length us, event | category | flops | bytes accessed | tf_op | source)
XLA Modules:
  0.0 813.6 jit_solution(16741182815726496434)
XLA Ops:
  7.9 7.2 reshape.486
  15.1 6.7 copy.43
  21.8 11.3 %copy.99 = bf16[512,8,8,128]{3,1,2,0:T(8,128)(2,1)} copy(bf16[512,8,8,128]{3,2,1,0:T(8,128)(2,1)} %bitcast.332) | data formatting | bytes 16777216
  33.1 11.6 %copy.45 = bf16[1024,4096]{1,0:T(8,128)(2,1)} copy(bf16[1024,4096]{0,1:T(8,128)(2,1)} %bitcast.324) | data formatting | bytes 16777216 | tf_op jit(solution)/shard_map/dot_general | solution.py:78
  47.3 6.6 fusion.30
  54.0 9.3 %fusion.39 = (pred[2,1024,1024]{1,2,0:T(8,128)(4,1)S(1)}, pred[2,1024,1024]{1,2,0:T(8,128)(4,1)}, pred[2,1024,1024]{1,2,0:T(8,128)(4,1)}) fusion(s32[1024]{0:T(1024)S(1)} %iota_add_fusion, pred[1024]{0:T(1024)(128)(4,1)S(1)} %get-tuple-element.47, pred[2,1024]{1,0:T(4,128)(4,1)S(1)} %get-tuple-element.10, pred[2,1024]{1,0:T(4,128)(4,1)S(1)} %get-tuple-element.32, ...), kind=kLoop, calls=%fused_computation.58 | loop fusion | flops 44040192 | bytes 6319104 | tf_op jit(solution)/shard_map/and | solution.py:39
  63.2 147.9 %all-gather.3.cloned.1.call-done = bf16[2,1024,4096]{2,1,0:T(8,128)(2,1)} async-done(((bf16[2,1024,2048]{2,1,0:T(8,128)(2,1)}), bf16[2,1024,4096]{2,1,0:T(8,128)(2,1)}) %all-gather.3.cloned.1.call-update) | async-done | bytes 16777232 | tf_op jit(solution)/shard_map/all_gather | solution.py:75
  211.1 13.1 %fusion.26 = f32[2,1024,2,2,128]{1,4,3,2,0:T(8,128)S(1)} fusion(bf16[2,2,128,4096,1]{3,2,1,0,4:T(8,128)(2,1)} %bitcast.336, bf16[2,1024,4096]{2,1,0:T(8,128)(2,1)} %all-gather.3.cloned.1.call-done), kind=kOutput, calls=%fused_computation.32 | convolution fusion | flops 8589934592 | bytes 25165824 | tf_op jit(solution)/shard_map/dot_general | solution.py:79
  239.5 21.0 %fusion.24 = f32[2,1024,8,128]{1,3,2,0:T(8,128)S(1)} fusion(bf16[8,128,4096,1]{2,1,0,3:T(8,128)(2,1)S(1)} %bitcast.335, bf16[2,1024,4096]{2,1,0:T(8,128)(2,1)} %all-gather.3.cloned.1.call-done), kind=kOutput, calls=%fused_computation.30 | convolution fusion | flops 17179869184 | bytes 33554432 | tf_op jit(solution)/shard_map/dot_general | solution.py:78
  288.6 23.9 %fusion.6 = (f32[2,2,4,1024]{3,2,1,0:T(4,128)S(1)}, f32[2,2,1024,1024,4]{3,2,4,1,0:T(8,128)}) fusion(pred[2,1024,1024]{1,2,0:T(8,128)(4,1)S(1)} %get-tuple-element.29, bf16[2,1024,2,4,128]{4,1,3,2,0:T(8,128)(2,1)S(1)} %pad_maximum_fusion, bf16[2,1024,2,64]{1,3,2,0:T(8,128)(2,1)S(1)} %get-tuple-element.22, bf16[2,1024,2,64]{1,3,2,0:T(8,128)(2,1)S(1)} %get-tuple-element.21), kind=kOutput, calls=%fused_computation.13 | convolution fusion | flops 4347379712 | bytes 74514432 | tf_op jit(solution)/shard_map/rqhgd,rkhd->rhgqk/dot_general | solution.py:49
  318.7 72.6 %all-gather = f32[32,4,2,2,128]{4,1,3,2,0:T(4,128)S(1)} all-gather(f32[2,4,2,2,128]{4,1,3,2,0:T(4,128)S(1)} %fusion.76), channel_id=2, replica_groups=mesh['grp'=2,'seq'=8,'tp'=2] {'grp','seq'}, dimensions={0}, use_global_device_ids=true | all-gather | bytes 278528 | tf_op jit(solution)/shard_map/all_gather | solution.py:127
  403.8 25.6 %fusion.7 = (f32[2,2,4,1024]{3,2,1,0:T(4,128)S(1)}, f32[2,2,1024,1024,4]{3,2,4,1,0:T(8,128)}) fusion(pred[2,1024,1024]{1,2,0:T(8,128)(4,1)} %get-tuple-element.31, bf16[2,1024,2,4,128]{4,1,3,2,0:T(8,128)(2,1)S(1)} %copy-done.1, bf16[2,1024,2,2,128]{1,4,3,2,0:T(8,128)(2,1)} %collective-permute-done), kind=kOutput, calls=%fused_computation.14 | convolution fusion | flops 4345282560 | bytes 74514432 | tf_op jit(solution)/shard_map/rqhgd,rkhd->rhgqk/dot_general | solution.py:49
  429.4 25.0 %fusion.8 = (f32[2,2,4,1024]{3,2,1,0:T(4,128)S(1)}, f32[2,2,1024,1024,4]{3,2,4,1,0:T(8,128)}) fusion(pred[2,1024,1024]{1,2,0:T(8,128)(4,1)S(1)} %copy-done.3, bf16[2,1024,2,4,128]{4,1,3,2,0:T(8,128)(2,1)S(1)} %copy-done.1, bf16[2,1024,2,2,128]{1,4,3,2,0:T(8,128)(2,1)} %collective-permute-done.2), kind=kOutput, calls=%fused_computation.15 | convolution fusion | flops 4345282560 | bytes 74514432 | tf_op jit(solution)/shard_map/rqhgd,rkhd->rhgqk/dot_general | solution.py:49
  454.4 37.3 %collective-permute-done.1 = bf16[2,2048,2,2,128]{1,4,3,2,0:T(8,128)(2,1)} collective-permute-done((bf16[2,2048,2,2,128]{1,4,3,2,0:T(8,128)(2,1)}, bf16[2,2048,2,2,128]{1,4,3,2,0:T(8,128)(2,1)}, u32[]{:S(2)}, u32[]{:S(2)}) %collective-permute-start.1) | collective-permute-done | bytes 4194336 | tf_op jit(solution)/shard_map/ppermute | solution.py:15
  491.7 48.3 %fusion = (f32[2,2,4,1024]{3,2,1,0:T(4,128)S(1)}, f32[2,2,2048,1024,4]{3,2,4,1,0:T(8,128)}) fusion(pred[2,1024,2048]{1,2,0:T(8,128)(4,1)} %fusion.30, bf16[2,1024,2,4,128]{4,1,3,2,0:T(8,128)(2,1)} %copy-done, bf16[2,2048,2,2,128]{1,4,3,2,0:T(8,128)(2,1)} %collective-permute-done.1), kind=kOutput, calls=%fused_computation.2 | convolution fusion | flops 8690581504 | bytes 144769024 | tf_op jit(solution)/shard_map/rqhgd,rkhd->rhgqk/dot_general | solution.py:49
  540.0 21.7 %fusion.9 = f32[2,2,4,1024]{3,2,1,0:T(4,128)S(1)} fusion(f32[2,2,1024,1024,4]{3,2,4,1,0:T(8,128)} %get-tuple-element.44, f32[2,2,4,1024]{3,2,1,0:T(4,128)S(1)} %get-tuple-element.25, pred[2,1024,1024]{1,2,0:T(8,128)(4,1)S(1)} %get-tuple-element.29), kind=kLoop, calls=%fused_computation.16 | loop fusion | flops 83869696 | bytes 69337088 | tf_op jit(solution)/shard_map/reduce_sum | solution.py:59
  561.8 29.2 %fusion.19 = f32[2,2,4,1024,128]{3,4,2,1,0:T(8,128)} fusion(f32[2,2,1024,1024,4]{3,2,4,1,0:T(8,128)} %get-tuple-element.44, f32[2,2,4,1024]{3,2,1,0:T(4,128)S(1)} %get-tuple-element.25, pred[2,1024,1024]{1,2,0:T(8,128)(4,1)S(1)} %get-tuple-element.29, f32[2,1024,2,2,128]{1,4,3,2,0:T(8,128)} %copy-done.6), kind=kOutput, calls=%fused_computation.24 | convolution fusion | flops 4378853376 | bytes 78708736 | tf_op jit(solution)/shard_map/rhgqk,rkhd->rhgqd/dot_general | solution.py:61
  595.9 21.7 %fusion.11 = f32[2,2,4,1024]{3,2,1,0:T(4,128)S(1)} fusion(f32[2,2,1024,1024,4]{3,2,4,1,0:T(8,128)} %get-tuple-element.42, f32[2,2,4,1024]{3,2,1,0:T(4,128)S(1)} %get-tuple-element.18, pred[2,1024,1024]{1,2,0:T(8,128)(4,1)S(1)} %copy-done.5), kind=kLoop, calls=%fused_computation.18 | loop fusion | flops 83869696 | bytes 69337088 | tf_op jit(solution)/shard_map/reduce_sum | solution.py:59
  617.5 42.6 %fusion.1 = f32[2,2,4,1024]{3,2,1,0:T(4,128)S(1)} fusion(f32[2,2,2048,1024,4]{3,2,4,1,0:T(8,128)} %get-tuple-element.40, f32[2,2,4,1024]{3,2,1,0:T(4,128)S(1)} %get-tuple-element.17, pred[2,1024,2048]{1,2,0:T(8,128)(4,1)} %fusion.30), kind=kLoop, calls=%fused_computation.3 | loop fusion | flops 167755776 | bytes 138543104 | tf_op jit(solution)/shard_map/reduce_sum | solution.py:59
  660.2 21.7 %fusion.13 = f32[2,2,4,1024]{3,2,1,0:T(4,128)S(1)} fusion(f32[2,2,1024,1024,4]{3,2,4,1,0:T(8,128)} %get-tuple-element.38, f32[2,2,4,1024]{3,2,1,0:T(4,128)S(1)} %get-tuple-element.16, pred[2,1024,1024]{1,2,0:T(8,128)(4,1)S(1)} %copy-done.4), kind=kLoop, calls=%fused_computation.20 | loop fusion | flops 83869696 | bytes 69337088 | tf_op jit(solution)/shard_map/reduce_sum | solution.py:59
  682.0 29.0 %fusion.17 = f32[2,2,4,1024,128]{3,4,2,1,0:T(8,128)} fusion(f32[2,2,1024,1024,4]{3,2,4,1,0:T(8,128)} %get-tuple-element.42, f32[2,2,4,1024]{3,2,1,0:T(4,128)S(1)} %get-tuple-element.18, pred[2,1024,1024]{1,2,0:T(8,128)(4,1)} %get-tuple-element.31, bf16[2,1024,2,2,128]{1,4,3,2,0:T(8,128)(2,1)} %collective-permute-done), kind=kOutput, calls=%fused_computation.23 | convolution fusion | flops 4378853376 | bytes 78708736 | tf_op jit(solution)/shard_map/rhgqk,rkhd->rhgqd/dot_general | solution.py:61
  711.0 50.0 %fusion.3 = f32[2,2,4,1024,128]{3,4,2,1,0:T(8,128)} fusion(f32[2,2,2048,1024,4]{3,2,4,1,0:T(8,128)} %get-tuple-element.40, f32[2,2,4,1024]{3,2,1,0:T(4,128)S(1)} %get-tuple-element.17, pred[2,1024,2048]{1,2,0:T(8,128)(4,1)} %fusion.30, bf16[2,2048,2,2,128]{1,4,3,2,0:T(8,128)(2,1)} %collective-permute-done.1), kind=kOutput, calls=%fused_computation.11 | convolution fusion | flops 8757706752 | bytes 148963328 | tf_op jit(solution)/shard_map/rhgqk,rkhd->rhgqd/dot_general | solution.py:61
  761.0 35.3 %fusion.32 = bf16[2,1024,2,4,128]{1,4,3,2,0:T(8,128)(2,1)} fusion(f32[2,2,4,1024,128]{3,4,2,1,0:T(8,128)} %fusion.63, f32[2,2,4,1024,128]{3,4,2,1,0:T(8,128)} %fusion.3, f32[2,2,4,1024,128]{3,4,2,1,0:T(8,128)} %fusion.17, f32[2,2,4,1024,128]{3,4,2,1,0:T(8,128)} %fusion.19, f32[2,1024,2,4]{1,3,2,0:T(4,128)S(1)} %get-tuple-element.11, ...), kind=kOutput, calls=%fused_computation.46 | convolution fusion | flops 4401922048 | bytes 108462080 | tf_op jit(solution)/shard_map/rhgqk,rkhd->rhgqd/dot_general | solution.py:61
  796.3 6.2 copy.59
  (85 shorter events, 74.2 us)
Async XLA Ops:
  7.2 204.0 %all-gather.3.cloned.1.call-start = ((), (), s32[]{:S(2)}) async-start(), calls=%async_computation.1 | async-start | bytes 25165824 | tf_op jit(solution)/shard_map/all_gather | solution.py:75
  33.1 11.7 %copy-start.13 = (s32[2,4]{1,0:T(2,128)S(1)}, s32[2,4]{1,0:T(2,128)}, u32[]{:S(2)}) copy-start(s32[2,4]{1,0:T(2,128)} %param.9) | copy-start | bytes 100
  33.1 12.0 %copy-start.16 = (s32[2]{0:T(128)S(1)}, s32[2]{0:T(128)}, u32[]{:S(2)}) copy-start(s32[2]{0:T(128)} %param.8) | copy-start | bytes 28
  45.4 346.0 %copy-start.9 = (pred[2,1024,4]{1,2,0:T(4,128)(4,1)}, pred[2,1024,4]{1,2,0:T(4,128)(4,1)S(1)}, u32[]{:S(2)}) copy-start(pred[2,1024,4]{1,2,0:T(4,128)(4,1)S(1)} %get-tuple-element.26) | copy-start | bytes 24580
  45.5 228.2 %copy-start.11 = (pred[2,1024]{1,0:T(4,128)(4,1)}, pred[2,1024]{1,0:T(4,128)(4,1)S(1)}, u32[]{:S(2)}) copy-start(pred[2,1024]{1,0:T(4,128)(4,1)S(1)} %get-tuple-element.32) | copy-start | bytes 6148
  211.1 13.5 %copy-start.7 = (f32[1024,64]{0,1:T(8,128)S(1)}, f32[1024,64]{0,1:T(8,128)}, u32[]{:S(2)}) copy-start(f32[1024,64]{0,1:T(8,128)} %get-tuple-element.28) | copy-start | bytes 786436
  224.3 15.2 %copy-start.6 = (f32[2,1024,2,2,128]{1,4,3,2,0:T(8,128)}, f32[2,1024,2,2,128]{1,4,3,2,0:T(8,128)S(1)}, u32[]{:S(2)}) copy-start(f32[2,1024,2,2,128]{1,4,3,2,0:T(8,128)S(1)} %fusion.26) | copy-start | bytes 12582916
  224.3 15.2 %slice-start = ((s8[8388608]{0:T(1024)(128)(4,1)}), s8[4194304]{0:T(1024)(128)(4,1)S(1)}, s32[]{:S(2)}) async-start(s8[8388608]{0:T(1024)(128)(4,1)} %bitcast.333), calls=%async_computation.2 | async-start | bytes 8388608
  224.6 2.3 copy-start.2
  224.6 14.9 %slice-start.1 = ((s8[8388608]{0:T(1024)(128)(4,1)}), s8[4194304]{0:T(1024)(128)(4,1)S(1)}, s32[]{:S(2)}) async-start(s8[8388608]{0:T(1024)(128)(4,1)} %bitcast.333), calls=%async_computation.3 | async-start | bytes 8388608
  228.5 167.1 %collective-permute-start = (bf16[2,1024,2,2,128]{1,4,3,2,0:T(8,128)(2,1)}, bf16[2,1024,2,2,128]{1,4,3,2,0:T(8,128)(2,1)}, u32[]{:S(2)}, u32[]{:S(2)}) collective-permute-start(bf16[2,1024,2,2,128]{1,4,3,2,0:T(8,128)(2,1)} %pad_maximum_fusion.1), channel_id=1, source_target_pairs={{0,2},{2,4},{4,6},{6,8},{8,10},{10,12},{12,14},{14,16},{16,18},{18... | collective-permute-start | bytes 6291464 | tf_op jit(solution)/shard_map/ppermute | solution.py:15
  233.5 195.9 %collective-permute-start.2 = (bf16[2,1024,2,2,128]{1,4,3,2,0:T(8,128)(2,1)}, bf16[2,1024,2,2,128]{1,4,3,2,0:T(8,128)(2,1)}, u32[]{:S(2)}, u32[]{:S(2)}) collective-permute-start(bf16[2,1024,2,2,128]{1,4,3,2,0:T(8,128)(2,1)} %pad_maximum_fusion.1), channel_id=1, source_target_pairs={{0,8},{2,10},{4,12},{6,14},{8,16},{10,18},{12,20},{14,22},{16,24},... | collective-permute-start | bytes 6291464 | tf_op jit(solution)/shard_map/ppermute | solution.py:15
  276.9 35.6 %all-to-all-start = ((bf16[2,2,1,1,1024,256]{4,5,0,3,2,1:T(8,128)(2,1)}), bf16[2,2,1,1,1024,256]{4,5,0,3,2,1:T(8,128)(2,1)}, u32[]{:S(2)}, u32[]{:S(2)}) async-start(bf16[2,2,1,1,1024,256]{4,5,0,3,2,1:T(8,128)(2,1)} %copy.60), calls=%async_computation | async-start | bytes 4194304 | tf_op jit(solution)/shard_map/all_to_all | solution.py:151
  286.6 2.0 copy-start
  391.4 38.0 %copy-start.14 = (bf16[2,4,2,2,128]{4,1,3,2,0:T(4,128)(2,1)}, bf16[2,4,2,2,128]{4,1,3,2,0:T(4,128)(2,1)S(1)}, u32[]{:S(2)}) copy-start(bf16[2,4,2,2,128]{4,1,3,2,0:T(4,128)(2,1)S(1)} %reduce_sum.64) | copy-start | bytes 24580
  391.4 12.4 %copy-start.1 = (bf16[2,1024,2,4,128]{4,1,3,2,0:T(8,128)(2,1)S(1)}, bf16[2,1024,2,4,128]{4,1,3,2,0:T(8,128)(2,1)}, u32[]{:S(2)}) copy-start(bf16[2,1024,2,4,128]{4,1,3,2,0:T(8,128)(2,1)} %copy-done) | copy-start | bytes 12582916
  399.2 92.5 %collective-permute-start.1 = (bf16[2,2048,2,2,128]{1,4,3,2,0:T(8,128)(2,1)}, bf16[2,2048,2,2,128]{1,4,3,2,0:T(8,128)(2,1)}, u32[]{:S(2)}, u32[]{:S(2)}) collective-permute-start(bf16[2,2048,2,2,128]{1,4,3,2,0:T(8,128)(2,1)} %maximum_maximum_fusion), channel_id=1, source_target_pairs={{0,4},{2,6},{4,8},{6,10},{8,12},{10,14},{12,16},{14,18},{16,20},{1... | collective-permute-start | bytes 12582920 | tf_op jit(solution)/shard_map/ppermute | solution.py:15
  403.7 25.6 %copy-start.3 = (pred[2,1024,1024]{1,2,0:T(8,128)(4,1)S(1)}, pred[2,1024,1024]{1,2,0:T(8,128)(4,1)}, u32[]{:S(2)}) copy-start(pred[2,1024,1024]{1,2,0:T(8,128)(4,1)} %get-tuple-element.30) | copy-start | bytes 6291460
  561.7 29.3 %copy-start.8 = (f32[2,2,4,1024,4]{3,4,2,1,0:T(4,128)S(1)}, f32[2,2,4,1024,4]{3,4,2,1,0:T(4,128)}, u32[]{:S(2)}) copy-start(f32[2,2,4,1024,4]{3,4,2,1,0:T(4,128)} %get-tuple-element.36) | copy-start | bytes 786436
  561.7 29.3 %copy-start.10 = (pred[2,1024,4]{1,2,0:T(4,128)(4,1)S(1)}, pred[2,1024,4]{1,2,0:T(4,128)(4,1)}, u32[]{:S(2)}) copy-start(pred[2,1024,4]{1,2,0:T(4,128)(4,1)} %copy-done.9) | copy-start | bytes 24580
  561.7 29.5 %copy-start.15 = (bf16[2,4,2,2,128]{4,1,3,2,0:T(4,128)(2,1)S(1)}, bf16[2,4,2,2,128]{4,1,3,2,0:T(4,128)(2,1)}, u32[]{:S(2)}) copy-start(bf16[2,4,2,2,128]{4,1,3,2,0:T(4,128)(2,1)} %copy-done.14) | copy-start | bytes 24580
  591.0 4.9 copy-start.5
  617.5 42.7 %copy-start.4 = (pred[2,1024,1024]{1,2,0:T(8,128)(4,1)S(1)}, pred[2,1024,1024]{1,2,0:T(8,128)(4,1)}, u32[]{:S(2)}) copy-start(pred[2,1024,1024]{1,2,0:T(8,128)(4,1)} %get-tuple-element.30) | copy-start | bytes 6291460
  796.3 6.2 copy-start.12
Sparse Core Ops, SparseCore 0:
  9.5 201.5 all-gather.2
